TPU v7x, 768 devices: a whole 4x8x12 slice. The times are simulated.
768 devices in a mesh: occ: 16 (over y, x_hi), vir: 48 (over z, x_lo, core).
Axes of the slice: x: 4 (x_hi: 2, x_lo: 2; x = x_hi * 2 + x_lo), y: 8, z: 12, core: 2. Of those that a mesh axis runs over, the one named last changes fastest.
Arguments:
- amplitudes: bfloat16 [32, 32, 768, 768], P('occ', None, 'vir'), may hold values from -6 to 6
- integrals: bfloat16 [768, 768], P('vir'), may hold values from -0.21875 to 0.21875
- occ_fock: bfloat16 [32, 32], replicated, may hold values from -1 to 1
- amp_mask: int32 [48, 48], replicated, may hold values 0 or 1
- int_mask: int32 [48, 48], replicated, may hold values 0 or 1
- occ_energy: float32 [32], replicated, may hold values from -2 to -0.5
- vir_energy: float32 [768], replicated, may hold values from 0.5 to 4
Outputs:
- update: float32 [32, 32, 768, 768], P('occ', None, 'vir')
All inputs are finite; a program needn't handle non-finite values.
Results may differ from a plain program's by a relative error of at most 0.002.
Values may be sent and summed in bfloat16 or wider, within the bound.
A program may use at most 128 MiB of HBM per device.

v0:
```python
import jax
import jax.numpy as jnp
from jax import lax
from jax.sharding import PartitionSpec as P

VB = 16


def expand_rows(mask, first_block, blocks):
    rows_here = lax.dynamic_slice_in_dim(mask, first_block, blocks, 0)
    return jnp.repeat(jnp.repeat(rows_here, VB, axis=0), VB, axis=1).astype(jnp.bfloat16)


def local(amplitudes, integrals, occ_fock, amp_mask, int_mask, occ_energy, vir_energy):
    occ_rows, occ_all, vir_rows, vir_all = amplitudes.shape
    vir_start = lax.axis_index("vir") * vir_rows
    occ_start = lax.axis_index("occ") * occ_rows
    blocks = vir_rows // VB
    first_block = vir_start // VB
    masked = amplitudes * expand_rows(amp_mask, first_block, blocks)[None, None]
    masked_w = integrals * expand_rows(int_mask, first_block, blocks)
    flat_amps = masked.reshape(-1, vir_all)
    full_w = lax.all_gather(masked_w, "vir", axis=0, tiled=True)
    ladder = jnp.dot(flat_amps, full_w, preferred_element_type=jnp.float32)
    ladder = ladder.reshape(occ_rows, occ_all, vir_rows, vir_all)
    holes = jnp.einsum("ikab,kj->ijab", masked, occ_fock, preferred_element_type=jnp.float32)
    mixed = ladder + holes
    outgoing = mixed.astype(jnp.bfloat16)
    arrived = lax.all_to_all(
        lax.all_to_all(outgoing, "occ", split_axis=1, concat_axis=0, tiled=True),
        "vir",
        split_axis=3,
        concat_axis=2,
        tiled=True,
    )
    mirrored = arrived.transpose(1, 0, 3, 2).astype(jnp.float32)
    vir_here = lax.dynamic_slice_in_dim(vir_energy, vir_start, vir_rows, 0)
    occ_here = lax.dynamic_slice_in_dim(occ_energy, occ_start, occ_rows, 0)
    denominator = (
        vir_here[None, None, :, None]
        + vir_energy[None, None, None, :]
        - occ_here[:, None, None, None]
        - occ_energy[None, :, None, None]
    )
    return (mixed + mirrored) / denominator


def solution(mesh):
    in_specs = (P("occ", None, "vir", None), P("vir", None), P(), P(), P(), P(), P())
    out_specs = P("occ", None, "vir", None)
    return jax.shard_map(local, mesh=mesh, in_specs=in_specs, out_specs=out_specs, check_vma=False)
```

profile of v0, /device:TPU:1, one launch (start us, length us, event | category | flops | bytes accessed | tf_op | source)
XLA Modules:
  0.0 310.4 jit_solution(152159300503923513)
XLA Ops:
  6.5 0.0 copy-start
  6.5 0.0 all-gather.2.cloned.1.call-start
  6.5 0.7 convert_bitcast_fusion
  7.3 0.1 broadcast_in_dim.7
  7.3 0.1 convert_element_type.46
  7.4 1.4 broadcast_multiply_fusion.1
  8.8 0.0 all-gather.2.cloned.1.call-update
  8.8 0.1 broadcast_in_dim.6
  8.9 0.1 convert_element_type.43
  9.0 1.5 broadcast_multiply_fusion
  10.5 0.0 copy-done
  10.5 2.3 fusion.1
  12.9 101.5 %all-gather.2.cloned.1.call-done = bf16[768,768]{1,0:T(8,128)(2,1)} async-done(((bf16[16,768]{1,0:T(8,128)(2,1)}), bf16[768,768]{1,0:T(8,128)(2,1)}) %all-gather.2.cloned.1.call-update) | async-done | bytes 1179664 | tf_op jit(solution)/shard_map/all_gather | solution.py:23
  114.4 6.7 %fusion.5 = (bf16[2,32,16,768]{3,2,1,0:T(8,128)(2,1)S(1)}, f32[2,32,16,768]{3,2,1,0:T(8,128)}) fusion(f32[2,16,768,32]{2,3,1,0:T(8,128)} %fusion.1, bf16[2,32,16,768]{3,2,1,0:T(8,128)(2,1)S(1)} %broadcast_multiply_fusion, bf16[768,768]{1,0:T(8,128)(2,1)} %all-gather.2.cloned.1.call-done), kind=kOutput, calls=%fused_computation.13 | convolution fusion | flops 1209532416 | bytes 10616832 | tf_op jit(solution)/shard_map/dot_general | solution.py:24
  121.0 0.2 copy.49
  121.2 48.5 %all_to_all.27 = bf16[2,32,16,768]{3,2,0,1:T(8,128)(2,1)S(1)} all-to-all(bf16[2,32,16,768]{3,2,0,1:T(8,128)(2,1)S(1)} %copy.49), channel_id=1, replica_groups=mesh['occ'=16,'vir'=48] {'occ'}, dimensions={1} | all-to-all | bytes 3145728 | tf_op jit(solution)/shard_map/all_to_all | solution.py:30
  169.7 0.2 copy.51
  169.9 9.8 %copy.52 = bf16[32,2,16,768]{0,2,1,3:T(8,128)(2,1)} copy(bf16[32,2,16,768]{3,2,1,0:T(8,128)(2,1)S(1)} %bitcast.36) | data formatting | bytes 3145728 | tf_op jit(solution)/shard_map/all_to_all | solution.py:30
  179.7 9.3 %reshape.65 = bf16[48,2,8192]{2,1,0:T(2,128)(2,1)} reshape(bf16[768,2,16,32]{3,2,1,0:T(8,128)(2,1)} %bitcast.33) | data formatting | bytes 3145728
  189.0 0.0 copy-start.3
  189.0 0.0 copy-start.2
  189.0 9.2 %all-to-all-start.1 = ((bf16[48,2,8192]{2,1,0:T(2,128)(2,1)}), bf16[48,2,8192]{2,1,0:T(2,128)(2,1)S(1)}, u32[]{:S(2)}, u32[]{:S(2)}) async-start(bf16[48,2,8192]{2,1,0:T(2,128)(2,1)} %reshape.65), calls=%async_computation.1 | async-start | bytes 3145728 | tf_op jit(solution)/shard_map/all_to_all | solution.py:29
  198.2 0.0 copy-done.3
  198.2 0.1 dynamic_slice.15
  198.3 0.0 copy-done.2
  198.3 0.1 dynamic_slice.14
  198.4 0.1 broadcast_add_fusion
  198.4 0.1 broadcast_subtract_fusion
  198.5 58.6 %all-to-all-done.1 = bf16[48,2,8192]{2,1,0:T(2,128)(2,1)S(1)} async-done(((bf16[48,2,8192]{2,1,0:T(2,128)(2,1)}), bf16[48,2,8192]{2,1,0:T(2,128)(2,1)S(1)}, u32[]{:S(2)}, u32[]{:S(2)}) %all-to-all-start.1) | async-done | bytes 1572896 | tf_op jit(solution)/shard_map/all_to_all | solution.py:29
  257.1 5.4 %reshape.66 = bf16[768,2,16,32]{3,2,1,0:T(8,128)(2,1)} reshape(bf16[48,2,8192]{2,1,0:T(2,128)(2,1)S(1)} %all-to-all-done.1) | data formatting | bytes 3145728
  262.5 8.5 %copy.53 = bf16[32,2,16,768]{3,2,1,0:T(8,128)(2,1)S(1)} copy(bf16[32,2,16,768]{0,2,1,3:T(8,128)(2,1)} %bitcast.34) | data formatting | bytes 3145728 | tf_op jit(solution)/shard_map/all_to_all | solution.py:29
  271.0 6.1 %copy.54 = f32[32,2,16,768]{0,3,2,1:T(8,128)} copy(bf16[32,2,16,768]{3,2,1,0:T(8,128)(2,1)S(1)} %copy.53) | data formatting | bytes 4718592 | tf_op jit(solution)/shard_map/convert_element_type | solution.py:36
  277.1 11.0 %copy.55 = f32[32,2,48,16,16]{0,4,3,2,1:T(8,128)} copy(f32[32,2,48,16,16]{0,4,2,3,1:T(8,128)} %bitcast.31) | data formatting | bytes 6291456 | tf_op jit(solution)/shard_map/convert_element_type | solution.py:36
  288.1 0.0 copy-start.1
  288.1 11.0 %copy.56 = f32[32,2,768,16]{2,3,0,1:T(8,128)} copy(f32[32,2,768,16]{0,3,2,1:T(8,128)} %bitcast.32) | data formatting | bytes 6291456 | tf_op jit(solution)/shard_map/convert_element_type | solution.py:36
  299.1 0.0 copy-done.1
  299.1 4.4 %fusion = f32[2,32,16,768]{3,2,1,0:T(8,128)} fusion(f32[2,32,16,768]{3,2,1,0:T(8,128)S(1)} %copy-done.1, f32[32,2,768,16]{2,3,0,1:T(8,128)} %copy.56, f32[32]{0:T(128)S(1)} %copy-done.3, f32[2,16,768]{2,1,0:T(8,128)S(1)} %broadcast_subtract_fusion), kind=kLoop, calls=%fused_computation.1 | loop fusion | flops 2359296 | bytes 9535616 | tf_op jit(solution)/shard_map/div | solution.py:45
Async XLA Ops:
  6.5 4.0 %copy-start = (bf16[32,32]{1,0:T(8,128)(2,1)S(1)}, bf16[32,32]{1,0:T(8,128)(2,1)}, u32[]{:S(2)}) copy-start(bf16[32,32]{1,0:T(8,128)(2,1)} %param.9) | copy-start | bytes 6148
  6.5 107.8 %all-gather.2.cloned.1.call-start = ((), (), s32[]{:S(2)}) async-start(), calls=%async_computation.2 | async-start | bytes 1204224 | tf_op jit(solution)/shard_map/all_gather | solution.py:23
  189.0 9.2 %copy-start.3 = (f32[32]{0:T(128)S(1)}, f32[32]{0:T(128)}, u32[]{:S(2)}) copy-start(f32[32]{0:T(128)} %param.12) | copy-start | bytes 388
  189.0 9.3 %copy-start.2 = (f32[768]{0:T(1024)S(1)}, f32[768]{0:T(1024)}, u32[]{:S(2)}) copy-start(f32[768]{0:T(1024)} %param.13) | copy-start | bytes 9220
  189.0 68.1 %all-to-all-start.1 = ((bf16[48,2,8192]{2,1,0:T(2,128)(2,1)}), bf16[48,2,8192]{2,1,0:T(2,128)(2,1)S(1)}, u32[]{:S(2)}, u32[]{:S(2)}) async-start(bf16[48,2,8192]{2,1,0:T(2,128)(2,1)} %reshape.65), calls=%async_computation.1 | async-start | bytes 3145728 | tf_op jit(solution)/shard_map/all_to_all | solution.py:29
  288.1 11.0 %copy-start.1 = (f32[2,32,16,768]{3,2,1,0:T(8,128)S(1)}, f32[2,32,16,768]{3,2,1,0:T(8,128)}, u32[]{:S(2)}) copy-start(f32[2,32,16,768]{3,2,1,0:T(8,128)} %get-tuple-element.6) | copy-start | bytes 9437188
Sparse Core Ops, SparseCore 0:
  9.8 104.4 all-gather.1
where the time goes:
time: 311 us; the launch traced here: 310 us
  waiting for transfers between devices  160 us (51%)
  local copies, waits for them, and re-layouts  61.9 us (20%)
  blocking collectives  48.5 us (16%)
  between operations  13.5 us (4%)
  starting transfers between devices  9.22 us (3%)
  matrix products  9.01 us (3%)
  other arithmetic  8.18 us (3%)
    all_gather x1, waiting for transfers between devices, local(): full_w = lax.all_gather(masked_w, 'vir', axis=0, tiled=True)  102 us
    all_to_all x1, waiting for transfers between devices, local(): lax.all_to_all(lax.all_to_all(outgoing, 'occ', split_axis=1, concat_axis=...  58.6 us
    all_to_all x1, blocking collectives, local(): lax.all_to_all(outgoing, 'occ', split_axis=1, concat_axis=0, tiled=True)  48.5 us
    convert_element_type x3, local copies, waits for them, and re-layouts, local(): mirrored = arrived.transpose(1, 0, 3, 2).astype(jnp.float32)  28.1 us
    unnamed x10, local copies, waits for them, and re-layouts  14.7 us
    all_to_all x2, local copies, waits for them, and re-layouts, local(): lax.all_to_all(outgoing, 'occ', split_axis=1, concat_axis=0, tiled=True)  9.95 us
    all_to_all x1, starting transfers between devices, local(): lax.all_to_all(lax.all_to_all(outgoing, 'occ', split_axis=1, concat_axis=...  9.22 us
    all_to_all x1, local copies, waits for them, and re-layouts, local(): lax.all_to_all(lax.all_to_all(outgoing, 'occ', split_axis=1, concat_axis=...  8.5 us
  transfers between devices with their start and end apart: 2, of which 2 were waited for; matrix products, arithmetic and copies ran while one was open for 1% of the time, Pallas kernels for 0%

commit v1 on v0

v1 whole, which is shorter than its diff:
```python
import jax
import jax.numpy as jnp
from jax import lax
from jax.experimental import pallas as pl
from jax.experimental.pallas import tpu as pltpu
from jax.sharding import PartitionSpec as P

VB = 16
NO = 32
V = 768
N_OCC = 16
N_VIR = 48
N_Z = 12
N_DEV = N_OCC * N_VIR
MESH = pl.DeviceIdType.MESH
F32, BF16 = jnp.float32, jnp.bfloat16
ANY = pl.BlockSpec(memory_space=pl.ANY)
IN_VMEM = pl.BlockSpec(memory_space=pltpu.VMEM)
IN_SMEM = pl.BlockSpec(memory_space=pltpu.SMEM)

Z_ORDER = (1, 11, 2, 10, 3, 9, 4, 8, 5, 7, 6)


def gather_kernel(w_ref, full_ref, own_sem, z_send, z_recv, x_send, x_recv, c_send, c_recv, d_send, d_recv):
    me = lax.axis_index("vir")
    z, x, c = me // 4, (me // 2) % 2, me % 2
    x_peer, c_peer = z * 4 + (1 - x) * 2 + c, z * 4 + x * 2 + (1 - c)

    barrier = pltpu.get_barrier_semaphore()
    for dz in Z_ORDER:
        pl.semaphore_signal(barrier, inc=1, device_id={"vir": ((z + dz) % N_Z) * 4 + x * 2 + c}, device_id_type=MESH)
    for peer in (x_peer, c_peer):
        pl.semaphore_signal(barrier, inc=1, device_id={"vir": peer}, device_id_type=MESH)
    pl.semaphore_wait(barrier, N_Z + 1)

    def send(src, slot, send_sem, recv_sem, peer):
        return pltpu.make_async_remote_copy(
            src_ref=src, dst_ref=full_ref.at[slot], send_sem=send_sem, recv_sem=recv_sem,
            device_id={"vir": peer}, device_id_type=MESH)

    sends = []

    def go(copy):
        copy.start()
        sends.append(copy)

    own = pltpu.make_async_copy(w_ref, full_ref.at[me], own_sem)
    own.start()
    for dz in Z_ORDER:
        go(send(w_ref, me, z_send.at[dz], z_recv.at[dz], ((z + dz) % N_Z) * 4 + x * 2 + c))
    go(send(w_ref, me, x_send.at[0], x_recv.at[0], x_peer))
    go(send(w_ref, me, c_send.at[0], c_recv.at[0], c_peer))

    def from_x(dz):
        slot = ((z - dz + N_Z) % N_Z) * 4 + (1 - x) * 2 + c
        send(full_ref.at[slot], slot, x_send.at[dz], x_recv.at[dz], x_peer).wait_recv()
        go(send(full_ref.at[slot], slot, d_send.at[dz], d_recv.at[dz], c_peer))

    before = 0
    for dz in Z_ORDER:
        slot = ((z - dz + N_Z) % N_Z) * 4 + x * 2 + c
        send(full_ref.at[slot], slot, z_send.at[dz], z_recv.at[dz], x_peer).wait_recv()
        go(send(full_ref.at[slot], slot, x_send.at[dz], x_recv.at[dz], x_peer))
        go(send(full_ref.at[slot], slot, c_send.at[dz], c_recv.at[dz], c_peer))
        from_x(before)
        before = dz
    from_x(before)
    for dz in range(N_Z):
        slot = ((z - dz + N_Z) % N_Z) * 4 + x * 2 + (1 - c)
        send(full_ref.at[slot], slot, c_send.at[dz], c_recv.at[dz], c_peer).wait_recv()
        slot = ((z - dz + N_Z) % N_Z) * 4 + (1 - x) * 2 + (1 - c)
        send(full_ref.at[slot], slot, d_send.at[dz], d_recv.at[dz], c_peer).wait_recv()
    for copy in sends:
        copy.wait_send()
    own.wait()


def gather(w):
    rows, cols = w.shape
    sem = pltpu.SemaphoreType.DMA((N_Z,))
    return pl.pallas_call(
        gather_kernel,
        out_shape=jax.ShapeDtypeStruct((N_VIR, rows, cols), w.dtype),
        in_specs=[IN_VMEM],
        out_specs=IN_VMEM,
        scratch_shapes=[pltpu.SemaphoreType.DMA] + [sem] * 8,
        compiler_params=pltpu.CompilerParams(collective_id=0, has_side_effects=True),
        name="gather_w",
    )(w)


def one_hot(rows, cols, hit):
    r = lax.broadcasted_iota(jnp.int32, (rows, cols), 0)
    c = lax.broadcasted_iota(jnp.int32, (rows, cols), 1)
    return jnp.where(hit(r, c), 1.0, 0.0).astype(BF16)


COLS = 256


def mix_kernel(amps_ref, w_ref, g_ref, amask_ref, imask_ref, mixed_ref, out_ref, masked, holes):
    me = lax.axis_index("vir")
    wide = one_hot(N_VIR, V, lambda r, c: r == c // VB)
    tall = one_hot(V, N_VIR, lambda r, c: r // VB == c)
    row = amask_ref[pl.ds(me, 1), :].astype(F32).astype(BF16)
    keep = jnp.dot(jnp.broadcast_to(row, (8, N_VIR)), wide, preferred_element_type=F32)[:1].astype(BF16)

    def mask_one(n, carry):
        i, j = n // NO, n % NO
        masked[i, pl.ds(j * VB, VB), :] = amps_ref[i, j] * keep
        return carry

    lax.fori_loop(0, 2 * NO, mask_one, 0, unroll=8)

    spread = one_hot(NO, NO * VB, lambda r, c: r == c // VB)
    g_wide = lax.dot_general(g_ref[...], spread, (((0,), (0,)), ((), ())), preferred_element_type=F32).astype(BF16)
    pick = one_hot(NO * VB, NO, lambda r, c: r // VB == c)
    kron = jnp.dot(pick, g_wide, preferred_element_type=F32)
    same = lax.broadcasted_iota(jnp.int32, kron.shape, 0) % VB == lax.broadcasted_iota(jnp.int32, kron.shape, 1) % VB
    holes[...] = jnp.where(same, kron, 0.0).astype(BF16)

    imask = imask_ref[...].astype(F32).astype(BF16)
    tall_mask = jnp.dot(tall, imask, preferred_element_type=F32).astype(BF16)
    for n in range(V // COLS):
        cols = slice(n * COLS, (n + 1) * COLS)
        w_keep = jnp.dot(tall_mask, wide[:, cols], preferred_element_type=F32).astype(BF16)
        w = w_ref[:, cols] * w_keep

        def rows_of(i, carry):
            both = jnp.dot(masked[i], w, preferred_element_type=F32)
            both = both + jnp.dot(holes[...], masked[i, :, cols], preferred_element_type=F32)
            mixed_ref[i, :, :, cols] = both.reshape(NO, VB, COLS)
            return carry

        lax.fori_loop(0, 2, rows_of, 0)

    low = lax.broadcasted_iota(jnp.int32, (N_VIR, 8, 128), 2) < 64

    def pack(p, carry):
        slabs = [mixed_ref[i, pl.ds(4 * p + 2 * h, 2)].reshape(2 * VB, V) for h in (0, 1) for i in (0, 1)]
        turned = jnp.concatenate(slabs, axis=0).T.reshape(N_VIR, 2, 8, 128)
        top, bottom = turned[:, 0], turned[:, 1]
        out_ref[2 * p] = jnp.where(low, top, pltpu.roll(bottom, 64, 2)).astype(BF16)
        out_ref[2 * p + 1] = jnp.where(low, pltpu.roll(top, 64, 2), bottom).astype(BF16)
        return carry

    lax.fori_loop(0, N_OCC // 2, pack, 0)


def mix(amps, w, g, amask, imask):
    return pl.pallas_call(
        mix_kernel,
        out_shape=(
            jax.ShapeDtypeStruct((2, NO, VB, V), F32),
            jax.ShapeDtypeStruct((N_OCC, N_VIR, 8, 128), BF16),
        ),
        in_specs=[IN_VMEM] * 5,
        out_specs=(IN_VMEM, IN_VMEM),
        scratch_shapes=[pltpu.VMEM((2, NO * VB, V), BF16), pltpu.VMEM((NO * VB, NO * VB), BF16)],
        compiler_params=pltpu.CompilerParams(vmem_limit_bytes=48 * 2**20),
        name="mix",
    )(amps, w, g, amask, imask)


def exchange_kernel(x_ref, o_ref, own_sem, send_sem, recv_sem):
    occ, vir = lax.axis_index("occ"), lax.axis_index("vir")
    me = occ * N_VIR + vir
    own = pltpu.make_async_copy(x_ref.at[me], o_ref.at[me], own_sem)
    own.start()

    def send(s, carry):
        to_occ = lax.rem(occ + s % N_OCC, N_OCC)
        to_vir = lax.rem(vir + ((s // N_OCC) * 19 + s * 7) % N_VIR, N_VIR)
        pltpu.make_async_remote_copy(
            src_ref=x_ref.at[to_occ * N_VIR + to_vir], dst_ref=o_ref.at[me], send_sem=send_sem, recv_sem=recv_sem,
            device_id=(to_occ, to_vir), device_id_type=MESH).start()
        return carry

    lax.fori_loop(1, N_DEV, send, 0)
    others = pl.ds(0, N_DEV - 1)
    pltpu.make_async_copy(x_ref.at[others], o_ref.at[others], recv_sem).wait()
    pltpu.make_async_copy(x_ref.at[others], o_ref.at[others], send_sem).wait()
    own.wait()


def exchange(tiles):
    return pl.pallas_call(
        exchange_kernel,
        out_shape=jax.ShapeDtypeStruct((N_DEV, 8, 128), BF16),
        in_specs=[IN_VMEM],
        out_specs=IN_VMEM,
        scratch_shapes=[pltpu.SemaphoreType.DMA] * 3,
        compiler_params=pltpu.CompilerParams(has_side_effects=True),
        name="exchange",
    )(tiles)


def finish_kernel(tiles_ref, mixed_ref, vir_sum_ref, occ_ref, out_ref):
    source = pl.program_id(0)
    occ = lax.axis_index("occ")
    x = tiles_ref[...].astype(F32).reshape(N_VIR // 8, 8, 8, 128)
    parts = [x[:, t] for t in range(8)]
    chunk = lax.broadcasted_iota(jnp.int32, parts[0].shape, 2) // VB
    for k in (1, 2, 4):
        low = (chunk // k) % 2 == 0
        for t in range(8):
            if t & k == 0:
                a, b = parts[t], parts[t + k]
                parts[t] = jnp.where(low, a, pltpu.roll(b, VB * k, 2))
                parts[t + k] = jnp.where(low, pltpu.roll(a, 128 - VB * k, 2), b)
    for c in range(8):
        half, i, jj = c // 4, (c // 2) % 2, c % 2
        energy = occ_ref[2 * occ + jj] + occ_ref[2 * source + i]
        rows = slice(half * 8, half * 8 + 8)
        for g in range(N_VIR // 8):
            cols = slice(g * 128, g * 128 + 128)
            total = mixed_ref[jj, i, rows, cols] + parts[c][g]
            out_ref[jj, i, rows, cols] = total / (vir_sum_ref[rows, cols] - energy)


def finish(tiles, mixed, vir_sum, occ_energy):
    block = pl.BlockSpec((2, 2, VB, V), lambda s: (0, s, 0, 0))
    return pl.pallas_call(
        finish_kernel,
        out_shape=jax.ShapeDtypeStruct((2, NO, VB, V), F32),
        grid=(N_OCC,),
        in_specs=[
            pl.BlockSpec((N_VIR, 8, 128), lambda s: (s, 0, 0)),
            block,
            pl.BlockSpec((VB, V), lambda s: (0, 0)),
            IN_SMEM,
        ],
        out_specs=block,
        name="finish",
    )(tiles, mixed, vir_sum, occ_energy)


def local(amplitudes, integrals, occ_fock, amp_mask, int_mask, occ_energy, vir_energy):
    vir_here = lax.dynamic_slice_in_dim(vir_energy, lax.axis_index("vir") * VB, VB, 0)
    vir_sum = vir_here[:, None] + vir_energy[None, :]
    full_w = gather(integrals).reshape(V, V)
    mixed, outgoing = mix(amplitudes, full_w, occ_fock, amp_mask, int_mask)
    arrived = exchange(outgoing.reshape(N_DEV, 8, 128))
    return finish(arrived, mixed, vir_sum, occ_energy)


def solution(mesh):
    in_specs = (P("occ", None, "vir", None), P("vir", None), P(), P(), P(), P(), P())
    out_specs = P("occ", None, "vir", None)
    return jax.shard_map(local, mesh=mesh, in_specs=in_specs, out_specs=out_specs, check_vma=False)
```

time: 311 us -> 154 us (0.50)
  waiting for transfers between devices: 160 us -> 0 us
  Pallas kernels: 0 us -> 145 us
  local copies, waits for them, and re-layouts: 61.9 us -> 6.74 us
  blocking collectives: 48.5 us -> 0 us
  between operations: 13.5 us -> 0.03 us
  starting transfers between devices: 9.22 us -> 0 us
  matrix products: 9.01 us -> 0 us
  other arithmetic: 8.18 us -> 1.37 us
    pallas_call x0 -> x4, Pallas kernels: none -> 145 us  [the longest x1 84.1 us: exchange(): pl.pallas_call(exchange_kernel, out_shape=jax.ShapeDtypeStruct((N_DEV, 8,...]
    all_gather x1 -> x0, waiting for transfers between devices: 102 us -> none  [local(): full_w = lax.all_gather(masked_w, 'vir', axis=0, tiled=True)]
    all_to_all x1 -> x0, waiting for transfers between devices: 58.6 us -> none  [local(): lax.all_to_all(lax.all_to_all(outgoing, 'occ', split_axis=1, concat_axis=...]
    all_to_all x1 -> x0, blocking collectives: 48.5 us -> none  [local(): lax.all_to_all(outgoing, 'occ', split_axis=1, concat_axis=0, tiled=True)]
    convert_element_type x6 -> x0, local copies, waits for them, and re-layouts: 28.5 us -> none  [the longest x3 28.1 us: local(): mirrored = arrived.transpose(1, 0, 3, 2).astype(jnp.float32)]
    all_to_all x3 -> x0, local copies, waits for them, and re-layouts: 18.5 us -> none  [the longest x2 9.95 us: local(): lax.all_to_all(outgoing, 'occ', split_axis=1, concat_axis=0, tiled=True)]
    all_to_all x1 -> x0, starting transfers between devices: 9.22 us -> none  [local(): lax.all_to_all(lax.all_to_all(outgoing, 'occ', split_axis=1, concat_axis=...]
    dot_general x2 -> x0, matrix products: 9.01 us -> none  [the longest x1 6.67 us: local(): ladder = jnp.dot(flat_amps, full_w, preferred_element_type=jnp.float32)]
  transfers between devices with their start and end apart: 2 -> 0, of which waited for: 2 -> 0; matrix products, arithmetic and copies ran while one was open for 1% -> 0% of each run, Pallas kernels for 0% -> 0%
where the time goes in v1:
time: 154 us; the launch traced here: 153 us
  Pallas kernels  145 us (94%)
  local copies, waits for them, and re-layouts  6.74 us (4%)
    pallas_call x1, Pallas kernels, exchange(): pl.pallas_call(exchange_kernel, out_shape=jax.ShapeDtypeStruct((N_DEV, 8,...  84.1 us
    pallas_call x1, Pallas kernels, gather(): pl.pallas_call(gather_kernel, out_shape=jax.ShapeDtypeStruct((N_VIR, rows...  40.5 us
    pallas_call x1, Pallas kernels, finish(): pl.pallas_call(finish_kernel, out_shape=jax.ShapeDtypeStruct((2, NO, VB,...  12.1 us
    pallas_call x1, Pallas kernels, mix(): pl.pallas_call(mix_kernel, out_shape=(jax.ShapeDtypeStruct((2, NO, VB, V)...  8.46 us
    unnamed x12, local copies, waits for them, and re-layouts  5.98 us

profile of v1, /device:TPU:1, one launch (start us, length us, event | category | flops | bytes accessed | tf_op | source)
XLA Modules:
  0.0 153.3 jit_solution(11325888170042407162)
XLA Ops:
  0.0 0.8 dynamic_slice.3
  0.8 1.4 broadcast_add_fusion.vir_sum_ref
  2.1 40.5 %gather_w.1 = bf16[48,16,768]{2,1,0:T(8,128)(2,1)} custom-call(bf16[16,768]{1,0:T(8,128)(2,1)} %w_ref.1), custom_call_target="tpu_custom_call" | custom-call | tf_op jit(solution)/shard_map/gather_w/pallas_call | solution.py:81
  42.6 0.0 copy-start
  42.7 1.3 copy-done
  43.9 0.0 copy-start.2
  43.9 1.4 copy-done.2
  45.3 0.0 copy-start.3
  45.3 0.7 copy-done.3
  46.1 0.0 copy-start.4
  46.1 0.7 copy-done.4
  46.8 0.0 copy-start.5
  46.8 0.7 copy-done.5
  47.5 8.5 %mix.1 = (f32[2,32,16,768]{3,2,1,0:T(8,128)}, bf16[16,48,8,128]{3,2,1,0:T(8,128)(2,1)S(1)}) custom-call(bf16[2,32,16,768]{3,2,1,0:T(8,128)(2,1)S(1)} %copy-done.2, bf16[768,768]{1,0:T(8,128)(2,1)S(1)} %bitcast.2, bf16[32,32]{1,0:T(8,128)(2,1)S(1)} %copy-done.5, s32[48,48]{1,0:T(8,128)S(1)} %copy-done.3, s32[48,48]{1,0:T(8,128)S(1)} %copy-done.4), custom_call_target="tpu_custom_call" | custom-call | tf_op jit(solution)/shard_map/mix/pallas_call | solution.py:151
  56.0 0.0 copy-start.1
  56.0 1.1 copy-done.1
  57.1 84.1 %exchange.1.tiles_ref = bf16[768,8,128]{2,1,0:T(8,128)(2,1)} custom-call(bf16[768,8,128]{2,1,0:T(8,128)(2,1)} %bitcast.3), custom_call_target="tpu_custom_call" | custom-call | tf_op jit(solution)/shard_map/exchange/pallas_call | solution.py:187
  141.2 12.1 %finish.1 = f32[2,32,16,768]{3,2,1,0:T(8,128)} custom-call(bf16[768,8,128]{2,1,0:T(8,128)(2,1)} %exchange.1.tiles_ref, f32[2,32,16,768]{3,2,1,0:T(8,128)} %get-tuple-element.8.mixed_ref, f32[16,768]{1,0:T(8,128)} %broadcast_add_fusion.vir_sum_ref, f32[32]{0:T(128)} %occ_ref.1), custom_call_target="tpu_custom_call" | custom-call | tf_op jit(solution)/shard_map/finish/pallas_call | solution.py:223
Async XLA Ops:
  42.6 1.3 copy-start
  43.9 1.4 copy-start.2
  45.3 0.7 copy-start.3
  46.1 0.7 copy-start.4
  46.8 0.7 copy-start.5
  56.0 1.1 copy-start.1

commit v2 on v0

v2 whole, which is shorter than its diff:
```python
import jax
import jax.numpy as jnp
from jax import lax
from jax.experimental import pallas as pl
from jax.experimental.pallas import tpu as pltpu
from jax.sharding import PartitionSpec as P

VB = 16
NO = 32
V = 768
N_OCC = 16
N_VIR = 48
N_Z = 12
N_DEV = N_OCC * N_VIR
N_PAIR = N_Z // 2
ROWS = NO * VB
MESH = pl.DeviceIdType.MESH
F32, BF16 = jnp.float32, jnp.bfloat16
IN_HBM = pl.BlockSpec(memory_space=pltpu.HBM)
IN_VMEM = pl.BlockSpec(memory_space=pltpu.VMEM)

Z_ORDER = (1, 11, 2, 10, 3, 9, 4, 8, 5, 7, 6)
PAIR_ORDER = ((3,), (2, 4), (1, 5), (0,))


def one_hot(rows, cols, hit):
    r = lax.broadcasted_iota(jnp.int32, (rows, cols), 0)
    c = lax.broadcasted_iota(jnp.int32, (rows, cols), 1)
    return jnp.where(hit(r, c), 1.0, 0.0).astype(BF16)


def kernel(
    amps_hbm, w_hbm, g_hbm, amask_hbm, imask_hbm, num_ref,
    amps, g, amask, imask, full, masked, holes, tall_mask, tiles, arrived,
    in_sem, z_send, z_recv, x_send, x_recv, c_send, c_recv, d_send, d_recv, entered, out_sem, tile_sem, own_sem,
):
    occ, me = lax.axis_index("occ"), lax.axis_index("vir")
    flat = occ * N_VIR + me
    z, x, c = me // 4, (me // 2) % 2, me % 2
    zp, odd = z // 2, z % 2
    x_peer, c_peer = z * 4 + (1 - x) * 2 + c, z * 4 + x * 2 + (1 - c)

    pairs = ((w_hbm, full.at[me]), (amps_hbm, amps), (amask_hbm, amask), (g_hbm, g), (imask_hbm, imask))
    loads = [pltpu.make_async_copy(src, dst, in_sem.at[n]) for n, (src, dst) in enumerate(pairs)]
    for load in loads:
        load.start()

    barrier = pltpu.get_barrier_semaphore()

    def greet_vir(s, carry):
        pl.semaphore_signal(barrier, inc=1, device_id=(occ, (me + s) % N_VIR), device_id_type=MESH)
        return carry

    def greet_occ(s, carry):
        pl.semaphore_signal(barrier, inc=1, device_id=((occ + s) % N_OCC, me), device_id_type=MESH)
        return carry

    def pass_on(s, carry):
        pl.semaphore_signal(entered, inc=1, device_id=((occ + s) % N_OCC, me), device_id_type=MESH)
        return carry

    lax.fori_loop(1, N_VIR, greet_vir, 0)
    lax.fori_loop(1, N_OCC, greet_occ, 0)
    pl.semaphore_wait(barrier, N_VIR + N_OCC - 2)
    lax.fori_loop(1, N_OCC, pass_on, 0)

    def send(slot, send_sem, recv_sem, peer):
        return pltpu.make_async_remote_copy(
            src_ref=full.at[slot], dst_ref=full.at[slot], send_sem=send_sem, recv_sem=recv_sem,
            device_id={"vir": peer}, device_id_type=MESH)

    sends = []

    def go(copy):
        copy.start()
        sends.append(copy)

    loads[0].wait()
    for dz in reversed(Z_ORDER):
        go(send(me, z_send.at[dz], z_recv.at[dz], ((z + dz) % N_Z) * 4 + x * 2 + c))
    go(send(me, x_send.at[0], x_recv.at[0], x_peer))
    go(send(me, c_send.at[0], c_recv.at[0], c_peer))

    def from_x(dz):
        slot = ((z - dz + N_Z) % N_Z) * 4 + (1 - x) * 2 + c
        send(slot, x_send.at[dz], x_recv.at[dz], x_peer).wait_recv()
        go(send(slot, d_send.at[dz], d_recv.at[dz], c_peer))

    def mask_amps():
        loads[1].wait()
        loads[2].wait()
        wide = one_hot(N_VIR, V, lambda r, c: r == c // VB)
        row = amask[pl.ds(me, 1), :].astype(F32).astype(BF16)
        keep = jnp.dot(jnp.broadcast_to(row, (8, N_VIR)), wide, preferred_element_type=F32)[:1].astype(BF16)

        def mask_one(n, carry):
            i, j = n // NO, n % NO
            masked[i, pl.ds(j * VB, VB), :] = amps[i, j] * keep
            return carry

        lax.fori_loop(0, 2 * NO, mask_one, 0, unroll=8)

    def make_holes():
        loads[3].wait()
        loads[4].wait()
        spread = one_hot(NO, ROWS, lambda r, c: r == c // VB)
        g_wide = lax.dot_general(g[...], spread, (((0,), (0,)), ((), ())), preferred_element_type=F32).astype(BF16)
        pick = one_hot(ROWS, NO, lambda r, c: r // VB == c)
        kron = jnp.dot(pick, g_wide, preferred_element_type=F32)
        same = lax.broadcasted_iota(jnp.int32, kron.shape, 0) % VB == lax.broadcasted_iota(jnp.int32, kron.shape, 1) % VB
        holes[...] = jnp.where(same, kron, 0.0).astype(BF16)
        tall = one_hot(V, N_VIR, lambda r, c: r // VB == c)
        tall_mask[...] = jnp.dot(tall, imask[...].astype(F32).astype(BF16), preferred_element_type=F32).astype(BF16)

    def add_holes(i):
        def tile(n, carry):
            cols = pl.ds(pl.multiple_of(n * 128, 128), 128)
            part = jnp.dot(holes[...], masked[i, :, cols], preferred_element_type=F32)
            num_ref[i, :, :, cols] = part.reshape(NO, VB, 128)
            return carry

        lax.fori_loop(0, N_PAIR, tile, 0)

    work = {1: mask_amps, 2: make_holes, 3: lambda: add_holes(0), 4: lambda: add_holes(1)}
    before = 0
    for dz in Z_ORDER:
        slot = ((z - dz + N_Z) % N_Z) * 4 + x * 2 + c
        send(slot, z_send.at[dz], z_recv.at[dz], x_peer).wait_recv()
        go(send(slot, x_send.at[dz], x_recv.at[dz], x_peer))
        go(send(slot, c_send.at[dz], c_recv.at[dz], c_peer))
        from_x(before)
        before = dz
        if dz in work:
            work[dz]()
    from_x(before)
    for dz in range(N_Z):
        slot = ((z - dz + N_Z) % N_Z) * 4 + x * 2 + (1 - c)
        send(slot, c_send.at[dz], c_recv.at[dz], c_peer).wait_recv()
        slot = ((z - dz + N_Z) % N_Z) * 4 + (1 - x) * 2 + (1 - c)
        send(slot, d_send.at[dz], d_recv.at[dz], c_peer).wait_recv()

    low = lax.broadcasted_iota(jnp.int32, (8, 8, 128), 2) < 64

    def make_tiles(q):
        cols = pl.ds(pl.multiple_of(q * 128, 128), 128)
        wide = one_hot(N_VIR, 128, lambda r, c: r == q * 8 + c // VB)
        w = full[:, :, cols].reshape(V, 128) * jnp.dot(tall_mask[...], wide, preferred_element_type=F32).astype(BF16)

        def ladder(i, carry):
            part = jnp.dot(masked[i], w, preferred_element_type=F32)
            num_ref[i, :, :, cols] += part.reshape(NO, VB, 128)
            return carry

        lax.fori_loop(0, 2, ladder, 0)

        def pack(p, carry):
            slabs = [num_ref[i, pl.ds(4 * p + 2 * h, 2), :, cols].reshape(2 * VB, 128) for h in (0, 1) for i in (0, 1)]
            turned = jnp.concatenate(slabs, axis=0).T.reshape(8, 2, 8, 128)
            top, bottom = turned[:, 0], turned[:, 1]
            tiles[pl.ds(2 * p * N_VIR + q * 8, 8)] = jnp.where(low, top, pltpu.roll(bottom, 64, 2)).astype(BF16)
            tiles[pl.ds((2 * p + 1) * N_VIR + q * 8, 8)] = jnp.where(low, pltpu.roll(top, 64, 2), bottom).astype(BF16)
            return carry

        lax.fori_loop(0, N_OCC // 2, pack, 0)

    def post(to_occ, to_vir, sem):
        pltpu.make_async_remote_copy(
            src_ref=tiles.at[to_occ * N_VIR + to_vir], dst_ref=arrived.at[flat], send_sem=out_sem, recv_sem=tile_sem.at[sem],
            device_id=(to_occ, to_vir), device_id_type=MESH).start()

    def lane(to_z, k):
        return to_z * 4 + ((x + k // 2) % 2) * 2 + (c + k) % 2

    for group in PAIR_ORDER:
        for dq in group:
            make_tiles((zp + dq) % N_PAIR)
        if group[0] == 3:
            pl.semaphore_wait(entered, N_OCC - 1)
        if group[0]:
            to_zs = [((zp + dq) % N_PAIR) * 2 + e for e in (0, 1) for dq in group]

            def post_pair(m, carry):
                to_occ = (occ + 8 + m * 5 + m // 16) % N_OCC
                for n, to_z in enumerate(to_zs):
                    post((to_occ + 4 * n) % N_OCC, lane(to_z, m // 16 + n), (to_z - z + N_Z) % N_Z)
                return carry

            lax.fori_loop(0, 64, post_pair, 0)
        else:
            other = zp * 2 + 1 - odd

            def post_near(m, carry):
                to_occ = (occ + 8 + m * 5 + m // 16) % N_OCC
                post(to_occ, lane(other, m // 16), (other - z + N_Z) % N_Z)
                return carry

            lax.fori_loop(0, 64, post_near, 0)

            def post_here(s, carry):
                for k in range(4):
                    post((occ + s) % N_OCC, lane(z, k), 0)
                return carry

            lax.fori_loop(1, N_OCC, post_here, 0)
            for k in range(1, 4):
                post(occ, lane(z, k), 0)
            own = pltpu.make_async_copy(tiles.at[flat], arrived.at[flat], own_sem)
            own.start()
            own.wait()

    for copy in sends:
        copy.wait_send()

    def wait_tiles(dz, count):
        part = arrived.at[pl.ds(0, count)]
        pltpu.make_async_copy(part, part, tile_sem.at[dz]).wait()

    chunk = lax.broadcasted_iota(jnp.int32, (8, 128), 1) // VB

    def add_mirror(q):
        cols = pl.ds(pl.multiple_of(q * 128, 128), 128)

        def one(source, carry):
            parts = [arrived[source * N_VIR + q * 8 + t].astype(F32) for t in range(8)]
            for k in (1, 2, 4):
                keep = (chunk // k) % 2 == 0
                for t in range(8):
                    if t & k == 0:
                        a, b = parts[t], parts[t + k]
                        parts[t] = jnp.where(keep, a, pltpu.roll(b, VB * k, 1))
                        parts[t + k] = jnp.where(keep, pltpu.roll(a, 128 - VB * k, 1), b)
            for n in range(8):
                half, i, jj = n // 4, (n // 2) % 2, n % 2
                num_ref[jj, 2 * source + i, half * 8 : half * 8 + 8, cols] += parts[n]
            return carry

        lax.fori_loop(0, N_OCC, one, 0, unroll=2)

    for group in PAIR_ORDER:
        for dq in group:
            q = (zp - dq + N_PAIR) % N_PAIR
            if dq:
                for e in (0, 1):
                    wait_tiles((z - (2 * q + e) + N_Z) % N_Z, 64)
            else:
                wait_tiles((z - (zp * 2 + 1 - odd) + N_Z) % N_Z, 64)
                wait_tiles(0, 63)
            add_mirror(q)

    others = tiles.at[pl.ds(0, N_DEV - 1)]
    pltpu.make_async_copy(others, others, out_sem).wait()


def local(amplitudes, integrals, occ_fock, amp_mask, int_mask, occ_energy, vir_energy):
    sem = pltpu.SemaphoreType.DMA
    total = pl.pallas_call(
        kernel,
        out_shape=jax.ShapeDtypeStruct(amplitudes.shape, F32),
        in_specs=[IN_HBM] * 5,
        out_specs=IN_VMEM,
        scratch_shapes=[
            pltpu.VMEM(amplitudes.shape, BF16),
            pltpu.VMEM(occ_fock.shape, BF16),
            pltpu.VMEM(amp_mask.shape, jnp.int32),
            pltpu.VMEM(int_mask.shape, jnp.int32),
            pltpu.VMEM((N_VIR, VB, V), BF16),
            pltpu.VMEM((2, ROWS, V), BF16),
            pltpu.VMEM((ROWS, ROWS), BF16),
            pltpu.VMEM((V, N_VIR), BF16),
            pltpu.VMEM((N_DEV, 8, 128), BF16),
            pltpu.VMEM((N_DEV, 8, 128), BF16),
            sem((5,)),
        ]
        + [sem((N_Z,))] * 8
        + [pltpu.SemaphoreType.REGULAR, sem, sem((N_Z,)), sem],
        compiler_params=pltpu.CompilerParams(collective_id=0, has_side_effects=True, vmem_limit_bytes=60 * 2**20),
        name="residual",
    )(amplitudes, integrals, occ_fock, amp_mask, int_mask)
    vir_here = lax.dynamic_slice_in_dim(vir_energy, lax.axis_index("vir") * VB, VB, 0)
    occ_here = lax.dynamic_slice_in_dim(occ_energy, lax.axis_index("occ") * 2, 2, 0)
    denominator = (
        vir_here[None, None, :, None]
        + vir_energy[None, None, None, :]
        - occ_here[:, None, None, None]
        - occ_energy[None, :, None, None]
    )
    return total / denominator


def solution(mesh):
    in_specs = (P("occ", None, "vir", None), P("vir", None), P(), P(), P(), P(), P())
    out_specs = P("occ", None, "vir", None)
    return jax.shard_map(local, mesh=mesh, in_specs=in_specs, out_specs=out_specs, check_vma=False)
```

time: 311 us -> 127 us (0.41)
  waiting for transfers between devices: 160 us -> 0 us
  Pallas kernels: 0 us -> 120 us
  local copies, waits for them, and re-layouts: 61.9 us -> 1.56 us
  blocking collectives: 48.5 us -> 0 us
  between operations: 13.5 us -> 0.02 us
  starting transfers between devices: 9.22 us -> 0 us
  matrix products: 9.01 us -> 0 us
  other arithmetic: 8.18 us -> 4.88 us
    pallas_call x0 -> x1, Pallas kernels: none -> 120 us  [local(): pl.pallas_call(kernel, out_shape=jax.ShapeDtypeStruct(amplitudes.shape, F...]
    all_gather x1 -> x0, waiting for transfers between devices: 102 us -> none  [local(): full_w = lax.all_gather(masked_w, 'vir', axis=0, tiled=True)]
    all_to_all x1 -> x0, waiting for transfers between devices: 58.6 us -> none  [local(): lax.all_to_all(lax.all_to_all(outgoing, 'occ', split_axis=1, concat_axis=...]
    all_to_all x1 -> x0, blocking collectives: 48.5 us -> none  [local(): lax.all_to_all(outgoing, 'occ', split_axis=1, concat_axis=0, tiled=True)]
    convert_element_type x6 -> x0, local copies, waits for them, and re-layouts: 28.5 us -> none  [the longest x3 28.1 us: local(): mirrored = arrived.transpose(1, 0, 3, 2).astype(jnp.float32)]
    all_to_all x3 -> x0, local copies, waits for them, and re-layouts: 18.5 us -> none  [the longest x2 9.95 us: local(): lax.all_to_all(outgoing, 'occ', split_axis=1, concat_axis=0, tiled=True)]
    unnamed x10 -> x2, local copies, waits for them, and re-layouts: 14.7 us -> 0.01 us
    all_to_all x1 -> x0, starting transfers between devices: 9.22 us -> none  [local(): lax.all_to_all(lax.all_to_all(outgoing, 'occ', split_axis=1, concat_axis=...]
  transfers between devices with their start and end apart: 2 -> 0, of which waited for: 2 -> 0; matrix products, arithmetic and copies ran while one was open for 1% -> 0% of each run, Pallas kernels for 0% -> 0%
where the time goes in v2:
time: 127 us
  Pallas kernels  120 us (94%)
  other arithmetic  4.88 us (4%)
  local copies, waits for them, and re-layouts  1.56 us (1%)
    pallas_call x1, Pallas kernels, local(): pl.pallas_call(kernel, out_shape=jax.ShapeDtypeStruct(amplitudes.shape, F...  120 us
    div x1, other arithmetic, local(): return total / denominator  4.04 us

profile of v2, /device:TPU:1, one launch (start us, length us, event | category | flops | bytes accessed | tf_op | source)
XLA Modules:
  0.0 126.7 jit_solution(7996770139441132843)
XLA Ops:
  0.0 0.0 copy-start
  0.0 0.8 dynamic_slice.7
  0.8 0.8 dynamic_slice.6
  1.6 0.8 broadcast_add_fusion
  2.3 0.1 broadcast_subtract_fusion
  2.4 120.2 %residual.1 = f32[2,32,16,768]{3,2,1,0:T(8,128)} custom-call(bf16[2,32,16,768]{3,2,1,0:T(8,128)(2,1)} %amps_hbm.1, bf16[16,768]{1,0:T(8,128)(2,1)} %w_hbm.1, bf16[32,32]{1,0:T(8,128)(2,1)} %g_hbm.1, s32[48,48]{1,0:T(8,128)} %amask_hbm.1, s32[48,48]{1,0:T(8,128)} %imask_hbm.1), custom_call_target="tpu_custom_call" | custom-call | tf_op jit(solution)/shard_map/residual/pallas_call | solution.py:256
  122.7 0.0 copy-done
  122.7 4.0 %subtract_divide_fusion = f32[2,32,16,768]{3,2,1,0:T(8,128)} fusion(f32[2,32,16,768]{3,2,1,0:T(8,128)} %residual.1, f32[32]{0:T(128)S(1)} %copy-done, f32[2,16,768]{2,1,0:T(8,128)S(1)} %broadcast_subtract_fusion), kind=kLoop, calls=%fused_computation | loop fusion | flops 1572864 | bytes 6389888 | tf_op jit(solution)/shard_map/div | solution.py:287
Async XLA Ops:
  0.0 122.7 %copy-start = (f32[32]{0:T(128)S(1)}, f32[32]{0:T(128)}, u32[]{:S(2)}) copy-start(f32[32]{0:T(128)} %param.12) | copy-start | bytes 388

commit v3 on v2

--- a/solution.py
+++ b/solution.py
@@ -16,10 +16,8 @@
 ROWS = NO * VB
 MESH = pl.DeviceIdType.MESH
 F32, BF16 = jnp.float32, jnp.bfloat16
-IN_HBM = pl.BlockSpec(memory_space=pltpu.HBM)
-IN_VMEM = pl.BlockSpec(memory_space=pltpu.VMEM)
-
-Z_ORDER = (1, 11, 2, 10, 3, 9, 4, 8, 5, 7, 6)
+IN_HBM = pl.BlockSpec(memory_space=pl.ANY)
+
 PAIR_ORDER = ((3,), (2, 4), (1, 5), (0,))
 
 
@@ -29,10 +27,14 @@
     return jnp.where(hit(r, c), 1.0, 0.0).astype(BF16)
 
 
+def near(n):
+    return (n % 2) * ((n + 1) // 2) + (1 - n % 2) * ((N_Z - n // 2) % N_Z)
+
+
 def kernel(
-    amps_hbm, w_hbm, g_hbm, amask_hbm, imask_hbm, num_ref,
-    amps, g, amask, imask, full, masked, holes, tall_mask, tiles, arrived,
-    in_sem, z_send, z_recv, x_send, x_recv, c_send, c_recv, d_send, d_recv, entered, out_sem, tile_sem, own_sem,
+    amps_hbm, w_hbm, g_hbm, amask_hbm, imask_hbm, vir_hbm, occ_energy, out_hbm,
+    num_ref, amps, g, amask, imask, energies, sums, twice, full, masked, holes, tall_mask, tiles, arrived,
+    in_sem, w_sem, put_sem, w_send, z_recv, x_recv, c_recv, d_recv, entered, out_sem, tile_sem, own_sem, done_sem,
 ):
     occ, me = lax.axis_index("occ"), lax.axis_index("vir")
     flat = occ * N_VIR + me
@@ -40,7 +42,10 @@
     zp, odd = z // 2, z % 2
     x_peer, c_peer = z * 4 + (1 - x) * 2 + c, z * 4 + x * 2 + (1 - c)
 
-    pairs = ((w_hbm, full.at[me]), (amps_hbm, amps), (amask_hbm, amask), (g_hbm, g), (imask_hbm, imask))
+    for q in range(2 * N_PAIR):
+        cols = slice((q % N_PAIR) * 128, (q % N_PAIR) * 128 + 128)
+        pltpu.make_async_copy(w_hbm.at[:, cols], twice.at[q], w_sem).start()
+    pairs = ((amps_hbm, amps), (amask_hbm, amask), (g_hbm, g), (imask_hbm, imask), (vir_hbm, energies))
     loads = [pltpu.make_async_copy(src, dst, in_sem.at[n]) for n, (src, dst) in enumerate(pairs)]
     for load in loads:
         load.start()
@@ -61,34 +66,10 @@
 
     lax.fori_loop(1, N_VIR, greet_vir, 0)
     lax.fori_loop(1, N_OCC, greet_occ, 0)
-    pl.semaphore_wait(barrier, N_VIR + N_OCC - 2)
-    lax.fori_loop(1, N_OCC, pass_on, 0)
-
-    def send(slot, send_sem, recv_sem, peer):
-        return pltpu.make_async_remote_copy(
-            src_ref=full.at[slot], dst_ref=full.at[slot], send_sem=send_sem, recv_sem=recv_sem,
-            device_id={"vir": peer}, device_id_type=MESH)
-
-    sends = []
-
-    def go(copy):
-        copy.start()
-        sends.append(copy)
-
-    loads[0].wait()
-    for dz in reversed(Z_ORDER):
-        go(send(me, z_send.at[dz], z_recv.at[dz], ((z + dz) % N_Z) * 4 + x * 2 + c))
-    go(send(me, x_send.at[0], x_recv.at[0], x_peer))
-    go(send(me, c_send.at[0], c_recv.at[0], c_peer))
-
-    def from_x(dz):
-        slot = ((z - dz + N_Z) % N_Z) * 4 + (1 - x) * 2 + c
-        send(slot, x_send.at[dz], x_recv.at[dz], x_peer).wait_recv()
-        go(send(slot, d_send.at[dz], d_recv.at[dz], c_peer))
 
     def mask_amps():
+        loads[0].wait()
         loads[1].wait()
-        loads[2].wait()
         wide = one_hot(N_VIR, V, lambda r, c: r == c // VB)
         row = amask[pl.ds(me, 1), :].astype(F32).astype(BF16)
         keep = jnp.dot(jnp.broadcast_to(row, (8, N_VIR)), wide, preferred_element_type=F32)[:1].astype(BF16)
@@ -101,8 +82,8 @@
         lax.fori_loop(0, 2 * NO, mask_one, 0, unroll=8)
 
     def make_holes():
+        loads[2].wait()
         loads[3].wait()
-        loads[4].wait()
         spread = one_hot(NO, ROWS, lambda r, c: r == c // VB)
         g_wide = lax.dot_general(g[...], spread, (((0,), (0,)), ((), ())), preferred_element_type=F32).astype(BF16)
         pick = one_hot(ROWS, NO, lambda r, c: r // VB == c)
@@ -121,30 +102,83 @@
 
         lax.fori_loop(0, N_PAIR, tile, 0)
 
-    work = {1: mask_amps, 2: make_holes, 3: lambda: add_holes(0), 4: lambda: add_holes(1)}
-    before = 0
-    for dz in Z_ORDER:
-        slot = ((z - dz + N_Z) % N_Z) * 4 + x * 2 + c
-        send(slot, z_send.at[dz], z_recv.at[dz], x_peer).wait_recv()
-        go(send(slot, x_send.at[dz], x_recv.at[dz], x_peer))
-        go(send(slot, c_send.at[dz], c_recv.at[dz], c_peer))
-        from_x(before)
-        before = dz
-        if dz in work:
-            work[dz]()
-    from_x(before)
-    for dz in range(N_Z):
-        slot = ((z - dz + N_Z) % N_Z) * 4 + x * 2 + (1 - c)
-        send(slot, c_send.at[dz], c_recv.at[dz], c_peer).wait_recv()
-        slot = ((z - dz + N_Z) % N_Z) * 4 + (1 - x) * 2 + (1 - c)
-        send(slot, d_send.at[dz], d_recv.at[dz], c_peer).wait_recv()
+    def add_energies():
+        loads[4].wait()
+        row = jnp.broadcast_to(energies[...].reshape(1, V), (VB, V))
+        here = me * VB + lax.broadcasted_iota(jnp.int32, (VB, V), 0) == lax.broadcasted_iota(jnp.int32, (VB, V), 1)
+        sums[...] = row + jnp.sum(jnp.where(here, row, 0.0), axis=1, keepdims=True)
+
+    mask_amps()
+    make_holes()
+    add_holes(0)
+    add_holes(1)
+    add_energies()
+    pltpu.make_async_copy(twice, twice, w_sem).wait()
+
+    pl.semaphore_wait(barrier, N_VIR + N_OCC - 2)
+    lax.fori_loop(1, N_OCC, pass_on, 0)
+
+    def part(ref, first, stage):
+        return ref.at[first] if stage == 0 else ref.at[pl.ds(first + 1, N_PAIR - 1)]
+
+    def own_to(peer, stage, recv_sem):
+        first = (peer // 8 + 3) % N_PAIR
+        pltpu.make_async_remote_copy(
+            src_ref=part(twice, first, stage), dst_ref=part(full.at[me], 0, stage), send_sem=w_send, recv_sem=recv_sem,
+            device_id={"vir": peer}, device_id_type=MESH).start()
+
+    def relay(slot, stage, recv_sem, peer):
+        here = part(full.at[slot], 0, stage)
+        return pltpu.make_async_remote_copy(
+            src_ref=here, dst_ref=here, send_sem=w_send, recv_sem=recv_sem,
+            device_id={"vir": peer}, device_id_type=MESH)
+
+    put = pltpu.make_async_copy(twice.at[pl.ds((zp + 3) % N_PAIR, N_PAIR)], full.at[me], put_sem)
+    put.start()
+    for stage in (0, 1):
+
+        def own_z(n, carry):
+            dz = near(N_Z - n)
+            own_to(((z + dz) % N_Z) * 4 + x * 2 + c, stage, z_recv.at[stage * N_Z + dz])
+            return carry
+
+        lax.fori_loop(1, N_Z, own_z, 0)
+        own_to(x_peer, stage, x_recv.at[stage * N_Z])
+        own_to(c_peer, stage, c_recv.at[stage * N_Z])
+
+    def gather_stage(stage):
+        def from_x(dz):
+            slot = ((z - dz + N_Z) % N_Z) * 4 + (1 - x) * 2 + c
+            relay(slot, stage, x_recv.at[stage * N_Z + dz], x_peer).wait_recv()
+            relay(slot, stage, d_recv.at[stage * N_Z + dz], c_peer).start()
+
+        def from_z(n, carry):
+            dz = near(n)
+            slot = ((z - dz + N_Z) % N_Z) * 4 + x * 2 + c
+            relay(slot, stage, z_recv.at[stage * N_Z + dz], x_peer).wait_recv()
+            relay(slot, stage, x_recv.at[stage * N_Z + dz], x_peer).start()
+            relay(slot, stage, c_recv.at[stage * N_Z + dz], c_peer).start()
+            from_x(near(n - 1))
+            return carry
+
+        def from_core(dz, carry):
+            slot = ((z - dz + N_Z) % N_Z) * 4 + x * 2 + (1 - c)
+            relay(slot, stage, c_recv.at[stage * N_Z + dz], c_peer).wait_recv()
+            slot = ((z - dz + N_Z) % N_Z) * 4 + (1 - x) * 2 + (1 - c)
+            relay(slot, stage, d_recv.at[stage * N_Z + dz], c_peer).wait_recv()
+            return carry
+
+        lax.fori_loop(1, N_Z, from_z, 0)
+        from_x(6)
+        lax.fori_loop(0, N_Z, from_core, 0)
 
     low = lax.broadcasted_iota(jnp.int32, (8, 8, 128), 2) < 64
 
-    def make_tiles(q):
+    def make_tiles(dq):
+        q = (zp + dq) % N_PAIR
         cols = pl.ds(pl.multiple_of(q * 128, 128), 128)
         wide = one_hot(N_VIR, 128, lambda r, c: r == q * 8 + c // VB)
-        w = full[:, :, cols].reshape(V, 128) * jnp.dot(tall_mask[...], wide, preferred_element_type=F32).astype(BF16)
+        w = full[:, (dq + 3) % N_PAIR].reshape(V, 128) * jnp.dot(tall_mask[...], wide, preferred_element_type=F32).astype(BF16)
 
         def ladder(i, carry):
             part = jnp.dot(masked[i], w, preferred_element_type=F32)
@@ -172,8 +206,13 @@
         return to_z * 4 + ((x + k // 2) % 2) * 2 + (c + k) % 2
 
     for group in PAIR_ORDER:
+        if group[0] == 3:
+            put.wait()
+            gather_stage(0)
+        elif group[0] == 2:
+            gather_stage(1)
         for dq in group:
-            make_tiles((zp + dq) % N_PAIR)
+            make_tiles(dq)
         if group[0] == 3:
             pl.semaphore_wait(entered, N_OCC - 1)
         if group[0]:
@@ -207,9 +246,6 @@
             own = pltpu.make_async_copy(tiles.at[flat], arrived.at[flat], own_sem)
             own.start()
             own.wait()
-
-    for copy in sends:
-        copy.wait_send()
 
     def wait_tiles(dz, count):
         part = arrived.at[pl.ds(0, count)]
@@ -231,10 +267,17 @@
                         parts[t + k] = jnp.where(keep, pltpu.roll(a, 128 - VB * k, 1), b)
             for n in range(8):
                 half, i, jj = n // 4, (n // 2) % 2, n % 2
-                num_ref[jj, 2 * source + i, half * 8 : half * 8 + 8, cols] += parts[n]
+                rows = slice(half * 8, half * 8 + 8)
+                total = num_ref[jj, 2 * source + i, rows, cols] + parts[n]
+                energy = occ_energy[2 * occ + jj] + occ_energy[2 * source + i]
+                num_ref[jj, 2 * source + i, rows, cols] = total / (sums[rows, cols] - energy)
             return carry
 
         lax.fori_loop(0, N_OCC, one, 0, unroll=2)
+
+    def write(q):
+        cols = pl.ds(pl.multiple_of(q * 128, 128), 128)
+        return pltpu.make_async_copy(num_ref.at[:, :, :, cols], out_hbm.at[:, :, :, cols], done_sem.at[q])
 
     for group in PAIR_ORDER:
         for dq in group:
@@ -246,45 +289,58 @@
                 wait_tiles((z - (zp * 2 + 1 - odd) + N_Z) % N_Z, 64)
                 wait_tiles(0, 63)
             add_mirror(q)
-
+            write(q).start()
+
+    for q in range(N_PAIR):
+        write(q).wait()
+    most = full.at[pl.ds(0, N_VIR - 1)]
+    pltpu.make_async_copy(most, most, w_send).wait()
     others = tiles.at[pl.ds(0, N_DEV - 1)]
     pltpu.make_async_copy(others, others, out_sem).wait()
 
 
+def copy_kernel(x_ref, o_ref):
+    o_ref[...] = x_ref[...]
+
+
 def local(amplitudes, integrals, occ_fock, amp_mask, int_mask, occ_energy, vir_energy):
     sem = pltpu.SemaphoreType.DMA
-    total = pl.pallas_call(
+    stages = sem((2 * N_Z,))
+    update = pl.pallas_call(
         kernel,
         out_shape=jax.ShapeDtypeStruct(amplitudes.shape, F32),
-        in_specs=[IN_HBM] * 5,
-        out_specs=IN_VMEM,
+        in_specs=[IN_HBM] * 6 + [pl.BlockSpec(memory_space=pltpu.SMEM)],
+        out_specs=IN_HBM,
         scratch_shapes=[
+            pltpu.VMEM(amplitudes.shape, F32),
             pltpu.VMEM(amplitudes.shape, BF16),
             pltpu.VMEM(occ_fock.shape, BF16),
             pltpu.VMEM(amp_mask.shape, jnp.int32),
             pltpu.VMEM(int_mask.shape, jnp.int32),
-            pltpu.VMEM((N_VIR, VB, V), BF16),
+            pltpu.VMEM(vir_energy.shape, F32),
+            pltpu.VMEM((VB, V), F32),
+            pltpu.VMEM((2 * N_PAIR, VB, 128), BF16),
+            pltpu.VMEM((N_VIR, N_PAIR, VB, 128), BF16),
             pltpu.VMEM((2, ROWS, V), BF16),
             pltpu.VMEM((ROWS, ROWS), BF16),
             pltpu.VMEM((V, N_VIR), BF16),
             pltpu.VMEM((N_DEV, 8, 128), BF16),
             pltpu.VMEM((N_DEV, 8, 128), BF16),
-            sem((5,)),
-        ]
-        + [sem((N_Z,))] * 8
-        + [pltpu.SemaphoreType.REGULAR, sem, sem((N_Z,)), sem],
+            sem((5,)), sem, sem, sem, stages, stages, stages, stages,
+            pltpu.SemaphoreType.REGULAR, sem, sem((N_Z,)), sem, sem((N_PAIR,)),
+        ],
         compiler_params=pltpu.CompilerParams(collective_id=0, has_side_effects=True, vmem_limit_bytes=60 * 2**20),
         name="residual",
-    )(amplitudes, integrals, occ_fock, amp_mask, int_mask)
-    vir_here = lax.dynamic_slice_in_dim(vir_energy, lax.axis_index("vir") * VB, VB, 0)
-    occ_here = lax.dynamic_slice_in_dim(occ_energy, lax.axis_index("occ") * 2, 2, 0)
-    denominator = (
-        vir_here[None, None, :, None]
-        + vir_energy[None, None, None, :]
-        - occ_here[:, None, None, None]
-        - occ_energy[None, :, None, None]
-    )
-    return total / denominator
+    )(amplitudes, integrals, occ_fock, amp_mask, int_mask, vir_energy, occ_energy)
+    block = pl.BlockSpec((2, 4, VB, V), lambda s: (0, s, 0, 0))
+    return pl.pallas_call(
+        copy_kernel,
+        out_shape=jax.ShapeDtypeStruct(amplitudes.shape, F32),
+        grid=(NO // 4,),
+        in_specs=[block],
+        out_specs=block,
+        name="place",
+    )(update)
 
 
 def solution(mesh):

time: 127 us -> 127 us (level)
  Pallas kernels: 120 us -> 127 us
  other arithmetic: 4.88 us -> 0 us
  local copies, waits for them, and re-layouts: 1.56 us -> 0 us
    pallas_call x0 -> x1, Pallas kernels: none -> 6.13 us  [local(): pl.pallas_call(copy_kernel, out_shape=jax.ShapeDtypeStruct(amplitudes.sha...]
    div x1 -> x0, other arithmetic: 4.04 us -> none  [local(): return total / denominator]
    dynamic_slice x2 -> x0, local copies, waits for them, and re-layouts: 1.56 us -> none  [the longest x1 0.8 us: local(): lax.dynamic_slice_in_dim(occ_energy, lax.axis_index('occ') * 2, 2, 0)]
where the time goes in v3:
time: 127 us
  Pallas kernels  127 us (100%)
    pallas_call x1, Pallas kernels, local(): pl.pallas_call(kernel, out_shape=jax.ShapeDtypeStruct(amplitudes.shape, F...  121 us
    pallas_call x1, Pallas kernels, local(): pl.pallas_call(copy_kernel, out_shape=jax.ShapeDtypeStruct(amplitudes.sha...  6.13 us

profile of v3, /device:TPU:1, one launch (start us, length us, event | category | flops | bytes accessed | tf_op | source)
XLA Modules:
  0.0 127.0 jit_solution(1949282381540973183)
XLA Ops:
  0.0 120.9 %residual.1.x_ref = f32[2,32,16,768]{3,2,1,0:T(8,128)} custom-call(bf16[2,32,16,768]{3,2,1,0:T(8,128)(2,1)} %amps_hbm.1, bf16[16,768]{1,0:T(8,128)(2,1)} %w_hbm.1, bf16[32,32]{1,0:T(8,128)(2,1)} %g_hbm.1, s32[48,48]{1,0:T(8,128)} %amask_hbm.1, s32[48,48]{1,0:T(8,128)} %imask_hbm.1, f32[768]{0:T(1024)} %vir_hbm.1, f32[32]{0:T(128)} %occ_energy.1), custom_call_target="tpu_custom_call" | custom-call | tf_op jit(solution)/shard_map/residual/pallas_call | solution.py:309
  120.9 6.1 %place.1 = f32[2,32,16,768]{3,2,1,0:T(8,128)} custom-call(f32[2,32,16,768]{3,2,1,0:T(8,128)} %residual.1.x_ref), custom_call_target="tpu_custom_call" | custom-call | tf_op jit(solution)/shard_map/place/pallas_call | solution.py:336

commit v4 on v3

--- a/solution.py
+++ b/solution.py
@@ -95,12 +95,12 @@
 
     def add_holes(i):
         def tile(n, carry):
-            cols = pl.ds(pl.multiple_of(n * 128, 128), 128)
+            cols = pl.ds(pl.multiple_of(n * 256, 256), 256)
             part = jnp.dot(holes[...], masked[i, :, cols], preferred_element_type=F32)
-            num_ref[i, :, :, cols] = part.reshape(NO, VB, 128)
-            return carry
-
-        lax.fori_loop(0, N_PAIR, tile, 0)
+            num_ref[i, :, :, cols] = part.reshape(NO, VB, 256)
+            return carry
+
+        lax.fori_loop(0, N_PAIR // 2, tile, 0)
 
     def add_energies():
         loads[4].wait()
@@ -138,7 +138,7 @@
     for stage in (0, 1):
 
         def own_z(n, carry):
-            dz = near(N_Z - n)
+            dz = near(n)
             own_to(((z + dz) % N_Z) * 4 + x * 2 + c, stage, z_recv.at[stage * N_Z + dz])
             return carry
 
@@ -199,11 +199,25 @@
 
     def post(to_occ, to_vir, sem):
         pltpu.make_async_remote_copy(
-            src_ref=tiles.at[to_occ * N_VIR + to_vir], dst_ref=arrived.at[flat], send_sem=out_sem, recv_sem=tile_sem.at[sem],
+            src_ref=tiles.at[to_occ * N_VIR + to_vir], dst_ref=mine, send_sem=out_sem, recv_sem=sem,
             device_id=(to_occ, to_vir), device_id_type=MESH).start()
 
-    def lane(to_z, k):
-        return to_z * 4 + ((x + k // 2) % 2) * 2 + (c + k) % 2
+    mine = arrived.at[flat]
+    peers = (me % 4, (1 - x) * 2 + c, x * 2 + (1 - c), (1 - x) * 2 + (1 - c))
+
+    def post_all(to_zs):
+        sems = [tile_sem.at[lax.rem(to_z - z + N_Z, N_Z)] for to_z in to_zs]
+
+        for k in range(4):
+            cols = [to_z * 4 + peers[(k + n) % 4] for n, to_z in enumerate(to_zs)]
+
+            def row(s, carry):
+                base = occ + s * 5 + 4 * k
+                for n, col in enumerate(cols):
+                    post(lax.rem(base + 4 * n, N_OCC), col, sems[n])
+                return carry
+
+            lax.fori_loop(0, N_OCC, row, 0, unroll=2)
 
     for group in PAIR_ORDER:
         if group[0] == 3:
@@ -216,34 +230,19 @@
         if group[0] == 3:
             pl.semaphore_wait(entered, N_OCC - 1)
         if group[0]:
-            to_zs = [((zp + dq) % N_PAIR) * 2 + e for e in (0, 1) for dq in group]
-
-            def post_pair(m, carry):
-                to_occ = (occ + 8 + m * 5 + m // 16) % N_OCC
-                for n, to_z in enumerate(to_zs):
-                    post((to_occ + 4 * n) % N_OCC, lane(to_z, m // 16 + n), (to_z - z + N_Z) % N_Z)
+            post_all([((zp + dq) % N_PAIR) * 2 + e for e in (0, 1) for dq in group])
+        else:
+            post_all([zp * 2 + 1 - odd])
+
+            def post_here(s, carry):
+                for peer in peers:
+                    post(lax.rem(occ + s, N_OCC), z * 4 + peer, tile_sem.at[0])
                 return carry
 
-            lax.fori_loop(0, 64, post_pair, 0)
-        else:
-            other = zp * 2 + 1 - odd
-
-            def post_near(m, carry):
-                to_occ = (occ + 8 + m * 5 + m // 16) % N_OCC
-                post(to_occ, lane(other, m // 16), (other - z + N_Z) % N_Z)
-                return carry
-
-            lax.fori_loop(0, 64, post_near, 0)
-
-            def post_here(s, carry):
-                for k in range(4):
-                    post((occ + s) % N_OCC, lane(z, k), 0)
-                return carry
-
-            lax.fori_loop(1, N_OCC, post_here, 0)
-            for k in range(1, 4):
-                post(occ, lane(z, k), 0)
-            own = pltpu.make_async_copy(tiles.at[flat], arrived.at[flat], own_sem)
+            lax.fori_loop(1, N_OCC, post_here, 0, unroll=3)
+            for peer in peers[1:]:
+                post(occ, z * 4 + peer, tile_sem.at[0])
+            own = pltpu.make_async_copy(tiles.at[flat], mine, own_sem)
             own.start()
             own.wait()
 
@@ -299,8 +298,21 @@
     pltpu.make_async_copy(others, others, out_sem).wait()
 
 
-def copy_kernel(x_ref, o_ref):
-    o_ref[...] = x_ref[...]
+N_PIECE = 16
+
+
+def copy_kernel(x_ref, o_ref, held, in_sem, out_sem):
+    rows = 2 * NO // N_PIECE
+    pieces = [(i, pl.ds(j, rows)) for i in (0, 1) for j in range(0, NO, rows)]
+    ins = [pltpu.make_async_copy(x_ref.at[p], held.at[p], in_sem.at[n]) for n, p in enumerate(pieces)]
+    outs = [pltpu.make_async_copy(held.at[p], o_ref.at[p], out_sem.at[n]) for n, p in enumerate(pieces)]
+    for copy in ins:
+        copy.start()
+    for arrival, copy in zip(ins, outs):
+        arrival.wait()
+        copy.start()
+    for copy in outs:
+        copy.wait()
 
 
 def local(amplitudes, integrals, occ_fock, amp_mask, int_mask, occ_energy, vir_energy):
@@ -332,13 +344,12 @@
         compiler_params=pltpu.CompilerParams(collective_id=0, has_side_effects=True, vmem_limit_bytes=60 * 2**20),
         name="residual",
     )(amplitudes, integrals, occ_fock, amp_mask, int_mask, vir_energy, occ_energy)
-    block = pl.BlockSpec((2, 4, VB, V), lambda s: (0, s, 0, 0))
     return pl.pallas_call(
         copy_kernel,
         out_shape=jax.ShapeDtypeStruct(amplitudes.shape, F32),
-        grid=(NO // 4,),
-        in_specs=[block],
-        out_specs=block,
+        in_specs=[IN_HBM],
+        out_specs=IN_HBM,
+        scratch_shapes=[pltpu.VMEM(amplitudes.shape, F32), sem((N_PIECE,)), sem((N_PIECE,))],
         name="place",
     )(update)
 

time: 127 us -> 118 us (0.929)
  Pallas kernels: 127 us -> 118 us
    pallas_call x1, Pallas kernels: 121 us -> 115 us  [local(): pl.pallas_call(kernel, out_shape=jax.ShapeDtypeStruct(amplitudes.shape, F...]
    pallas_call x1, Pallas kernels: 6.13 us -> 3.17 us  [local(): pl.pallas_call(copy_kernel, out_shape=jax.ShapeDtypeStruct(amplitudes.sha...]
where the time goes in v4:
time: 118 us
  Pallas kernels  118 us (100%)
    pallas_call x1, Pallas kernels, local(): pl.pallas_call(kernel, out_shape=jax.ShapeDtypeStruct(amplitudes.shape, F...  115 us
    pallas_call x1, Pallas kernels, local(): pl.pallas_call(copy_kernel, out_shape=jax.ShapeDtypeStruct(amplitudes.sha...  3.17 us

profile of v4, /device:TPU:1, one launch (start us, length us, event | category | flops | bytes accessed | tf_op | source)
XLA Modules:
  0.0 117.7 jit_solution(216365279252936494)
XLA Ops:
  0.0 114.5 %residual.1.x_ref = f32[2,32,16,768]{3,2,1,0:T(8,128)} custom-call(bf16[2,32,16,768]{3,2,1,0:T(8,128)(2,1)} %amps_hbm.1, bf16[16,768]{1,0:T(8,128)(2,1)} %w_hbm.1, bf16[32,32]{1,0:T(8,128)(2,1)} %g_hbm.1, s32[48,48]{1,0:T(8,128)} %amask_hbm.1, s32[48,48]{1,0:T(8,128)} %imask_hbm.1, f32[768]{0:T(1024)} %vir_hbm.1, f32[32]{0:T(128)} %occ_energy.1), custom_call_target="tpu_custom_call" | custom-call | tf_op jit(solution)/shard_map/residual/pallas_call | solution.py:321
  114.5 3.2 %place.1 = f32[2,32,16,768]{3,2,1,0:T(8,128)} custom-call(f32[2,32,16,768]{3,2,1,0:T(8,128)} %residual.1.x_ref), custom_call_target="tpu_custom_call" | custom-call | tf_op jit(solution)/shard_map/place/pallas_call | solution.py:347
